TPU v7x, 128 devices: a whole 4x4x4 slice. The times are simulated.
128 devices in a mesh: seq: 32 (over y, x, z_lo), mp: 4 (over z_hi, core).
Axes of the slice: x: 4, y: 4, z: 4 (z_hi: 2, z_lo: 2; z = z_hi * 2 + z_lo), core: 2. Of those that a mesh axis runs over, the one named last changes fastest.
Arguments:
- frames: bfloat16 [768, 250, 256], P('seq'), may hold values from -7.5 to 7.5
- intra_qkv: bfloat16 [256, 3, 256], P(None, None, 'mp'), may hold values from -20 to 20
- intra_out: bfloat16 [256, 256], P('mp'), may hold values from -0.375 to 0.375
- intra_up: bfloat16 [256, 1024], P(None, 'mp'), may hold values from -0.375 to 0.375
- intra_down: bfloat16 [1024, 256], P('mp'), may hold values from -0.1875 to 0.1875
- inter_qkv: bfloat16 [256, 3, 256], P(None, None, 'mp'), may hold values from -20 to 20
- inter_out: bfloat16 [256, 256], P('mp'), may hold values from -0.375 to 0.375
- inter_up: bfloat16 [256, 1024], P(None, 'mp'), may hold values from -0.375 to 0.375
- inter_down: bfloat16 [1024, 256], P('mp'), may hold values from -0.1875 to 0.1875
Outputs:
- margin_sum: bfloat16 [96000, 256], P('seq')
All inputs are finite; a program needn't handle non-finite values.
Results may differ from a plain program's by a relative error of at most 0.014.
Values may be sent and summed in bfloat16 or wider, within the bound.
No kernel may reach another device: no remote copies, remote signals or barrier semaphores. Data moves between devices by JAX's collectives and lax.ppermute only.
A program may use at most 128 MiB of HBM per device.

v0:
```python
import jax
import jax.numpy as jnp
from jax import lax
from jax.sharding import PartitionSpec as P

HEADS = 8
HD = 32
K = 250


def in_order(blocks, dim):
    lengths = list(blocks.shape[1:])
    lengths[dim] *= blocks.shape[0]
    return jnp.moveaxis(blocks, 0, dim).reshape(lengths)


def gather_together(arrays, axis, dims):
    vector = jnp.concatenate([a.reshape(-1) for a in arrays])
    lines, at, done = (lax.all_gather(vector, axis), 0, [])
    for a, dim in zip(arrays, dims):
        blocks = lines[:, at : at + a.size].reshape(-1, *a.shape)
        done.append(in_order(blocks, dim))
        at += a.size
    return tuple(done)


def passed_along(shard, axis, by):
    peers = lax.axis_size(axis)
    pairs = [(i, i + by) for i in range(peers) if 0 <= i + by < peers]
    return lax.ppermute(shard, axis, pairs)


def layer_norm(values):
    values = values.astype(jnp.float32)
    centre = values - jnp.mean(values, axis=-1, keepdims=True)
    spread = jnp.mean(centre * centre, axis=-1, keepdims=True)
    return (centre * lax.rsqrt(spread + 1e-05)).astype(jnp.bfloat16)


def attend(query_rows, key_rows, value_rows):
    factor = query_rows.shape[-1] ** (-0.5)
    scores = (
        jnp.einsum("bqhe,bkhe->bhqk", query_rows, key_rows, preferred_element_type=jnp.float32)
        * factor
    )
    scores = scores - jnp.max(scores, axis=-1, keepdims=True)
    weights = jnp.exp(scores)
    weights = (weights / jnp.sum(weights, axis=-1, keepdims=True)).astype(jnp.bfloat16)
    return jnp.einsum(
        "bhqk,bkhe->bqhe", weights, value_rows, preferred_element_type=jnp.float32
    ).astype(jnp.bfloat16)


def attend_rows(query_rows, key_rows, value_rows, per_step):
    blocks = query_rows.shape[0] // per_step
    stacked = tuple(
        (
            member.reshape((blocks, per_step) + member.shape[1:])
            for member in (query_rows, key_rows, value_rows)
        )
    )
    attended = lax.map(lambda pieces: attend(pieces[0], pieces[1], pieces[2]), stacked)
    return attended.reshape(query_rows.shape)


def whole_block(stream, qkv_weight, out_weight, up_weight, down_weight):
    normed = layer_norm(stream)
    projected = jnp.einsum(
        "pcd,dtj->tpcj", normed, qkv_weight, preferred_element_type=jnp.float32
    ).astype(jnp.bfloat16)
    projected = projected.reshape(3, stream.shape[0], stream.shape[1], HEADS, HD)
    attended = attend_rows(projected[0], projected[1], projected[2], 1)
    branch = jnp.einsum(
        "pche,hed->pcd",
        attended,
        out_weight.reshape(HEADS, HD, -1),
        preferred_element_type=jnp.float32,
    )
    middle = (stream.astype(jnp.float32) + branch).astype(jnp.bfloat16)
    normed = layer_norm(middle)
    hidden = jax.nn.relu(
        jnp.einsum("pcd,df->pcf", normed, up_weight, preferred_element_type=jnp.float32)
    ).astype(jnp.bfloat16)
    branch = jnp.einsum("pcf,fd->pcd", hidden, down_weight, preferred_element_type=jnp.float32)
    return (middle.astype(jnp.float32) + branch).astype(jnp.bfloat16)


def on_device(
    frames, intra_qkv, intra_out, intra_up, intra_down, inter_qkv, inter_out, inter_up, inter_down
):
    seq_count = lax.axis_size("seq")
    model_count = lax.axis_size("mp")
    intra_full = gather_together((intra_qkv, intra_out, intra_up, intra_down), "mp", (2, 0, 1, 0))
    span_count = frames.shape[0] // model_count
    own_spans = lax.dynamic_slice_in_dim(frames, lax.axis_index("mp") * span_count, span_count, 0)
    finished = whole_block(own_spans, intra_full[0], intra_full[1], intra_full[2], intra_full[3])
    stream = lax.all_gather(finished, "mp", axis=0, tiled=True)
    spread_devices = seq_count * model_count
    padded_len = (K + spread_devices - 1) // spread_devices * spread_devices
    full_weights = gather_together((inter_qkv, inter_out, inter_up, inter_down), "mp", (2, 0, 1, 0))
    per_device = padded_len // spread_devices
    arranged = jnp.pad(jnp.transpose(stream, (1, 0, 2)), ((0, padded_len - K), (0, 0), (0, 0)))
    arranged = arranged.reshape(
        seq_count, model_count, per_device, stream.shape[0], stream.shape[2]
    )
    mine = lax.dynamic_index_in_dim(arranged, lax.axis_index("mp"), 1, keepdims=False)
    mine = mine.reshape(seq_count * per_device, stream.shape[0], stream.shape[2])
    spread_rows = lax.all_to_all(mine, "seq", split_axis=0, concat_axis=1, tiled=True)
    spread_rows = whole_block(
        spread_rows, full_weights[0], full_weights[1], full_weights[2], full_weights[3]
    )
    returned = lax.all_to_all(spread_rows, "seq", split_axis=1, concat_axis=0, tiled=True)
    returned = returned.reshape(seq_count, 1, per_device, stream.shape[0], stream.shape[2])
    collected = lax.all_gather(returned, "mp", axis=1, tiled=True)
    collected = collected.reshape(padded_len, stream.shape[0], stream.shape[2])
    stream = jnp.transpose(collected[:K], (1, 0, 2))
    hop_len = K // 2
    tail_rows = stream[:, hop_len:]
    carried = passed_along(tail_rows[-1], "seq", 1)
    earlier = jnp.concatenate([carried[None], tail_rows[:-1]], axis=0)
    summed = stream[:, :hop_len].astype(jnp.float32) + earlier.astype(jnp.float32)
    return summed.astype(jnp.bfloat16).reshape(-1, stream.shape[2])


def solution(mesh):
    return jax.shard_map(
        on_device,
        mesh=mesh,
        in_specs=(
            P("seq", None, None),
            P(None, None, "mp"),
            P("mp", None),
            P(None, "mp"),
            P("mp", None),
            P(None, None, "mp"),
            P("mp", None),
            P(None, "mp"),
            P("mp", None),
        ),
        out_specs=P("seq", None),
        check_vma=False,
    )
```

profile of v0, /device:TPU:8, one launch (start us, length us, event | category | flops | bytes accessed | tf_op | source)
XLA Modules:
  0.0 260.5 jit_solution(12997414813802845133)
XLA Ops:
  17.4 20.4 %all-gather.10.cloned.1.call-done = bf16[786432]{0:T(1024)(128)(2,1)} async-done(((bf16[196608]{0:T(1024)(128)(2,1)}), bf16[786432]{0:T(1024)(128)(2,1)}) %all-gather.10.cloned.1.call-update) | async-done | bytes 1572880 | tf_op jit(solution)/shard_map/all_gather | solution.py:19
  37.8 2.0 reshape.242
  48.4 27.5 %while.20 = (s32[]{:T(128)}, bf16[6,1,250,8,32]{2,4,3,1,0:T(8,128)(2,1)}, bf16[6,1,250,8,32]{2,4,3,1,0:T(8,128)(2,1)}, bf16[6,1,250,8,32]{2,4,3,1,0:T(8,128)(2,1...) while((s32[]{:T(128)}, bf16[6,1,250,8,32]{2,4,3,1,0:T(8,128)(2,1)}, bf16[6,1,250,8,32]{2,4,3,1,0:T(8,128)(2,1)}, ...), condition=%wide.region_5.6_spmd, body=%wide.region_2.5_spmd.sunk | while | flops 99566496 | bytes 805573 | solution.py:62
  48.4 1.8 fusion.176
  50.3 2.7 %fusion.177 = bf16[6,1,250,8,32]{2,4,3,1,0:T(8,128)(2,1)} fusion(bf16[6,1,250,8,32]{2,4,3,1,0:T(8,128)(2,1)} %get-tuple-element.220, s32[]{:T(128)} %get-tuple-element.219, f32[8,250]{1,0:T(8,128)S(1)} %fusion.176, bf16[6,1,250,8,32]{2,4,3,1,0:T(8,128)(2,1)} %get-tuple-element.227, bf16[6,1,250,8,32]{2,4,3,1,0:T(8,128)(2,1)} %get-tuple-element.229, ...), kind=kOutput, calls=%fused_computation.7.clone.1 | convolution fusion | flops 66066248 | bytes 534336 | tf_op jit(solution)/shard_map/while/body/eval_jaxpr/bhqk,bkhe->bqhe/dot_general | solution.py:49
  54.9 2.7 %fusion.177 = bf16[6,1,250,8,32]{2,4,3,1,0:T(8,128)(2,1)} fusion(bf16[6,1,250,8,32]{2,4,3,1,0:T(8,128)(2,1)} %get-tuple-element.220, s32[]{:T(128)} %get-tuple-element.219, f32[8,250]{1,0:T(8,128)S(1)} %fusion.176, bf16[6,1,250,8,32]{2,4,3,1,0:T(8,128)(2,1)} %get-tuple-element.227, bf16[6,1,250,8,32]{2,4,3,1,0:T(8,128)(2,1)} %get-tuple-element.229, ...), kind=kOutput, calls=%fused_computation.7.clone.1 | convolution fusion | flops 66066248 | bytes 534336 | tf_op jit(solution)/shard_map/while/body/eval_jaxpr/bhqk,bkhe->bqhe/dot_general | solution.py:49
  57.6 1.8 fusion.176
  59.4 2.8 %fusion.177 = bf16[6,1,250,8,32]{2,4,3,1,0:T(8,128)(2,1)} fusion(bf16[6,1,250,8,32]{2,4,3,1,0:T(8,128)(2,1)} %get-tuple-element.220, s32[]{:T(128)} %get-tuple-element.219, f32[8,250]{1,0:T(8,128)S(1)} %fusion.176, bf16[6,1,250,8,32]{2,4,3,1,0:T(8,128)(2,1)} %get-tuple-element.227, bf16[6,1,250,8,32]{2,4,3,1,0:T(8,128)(2,1)} %get-tuple-element.229, ...), kind=kOutput, calls=%fused_computation.7.clone.1 | convolution fusion | flops 66066248 | bytes 534336 | tf_op jit(solution)/shard_map/while/body/eval_jaxpr/bhqk,bkhe->bqhe/dot_general | solution.py:49
  62.2 1.8 fusion.176
  64.1 2.8 %fusion.177 = bf16[6,1,250,8,32]{2,4,3,1,0:T(8,128)(2,1)} fusion(bf16[6,1,250,8,32]{2,4,3,1,0:T(8,128)(2,1)} %get-tuple-element.220, s32[]{:T(128)} %get-tuple-element.219, f32[8,250]{1,0:T(8,128)S(1)} %fusion.176, bf16[6,1,250,8,32]{2,4,3,1,0:T(8,128)(2,1)} %get-tuple-element.227, bf16[6,1,250,8,32]{2,4,3,1,0:T(8,128)(2,1)} %get-tuple-element.229, ...), kind=kOutput, calls=%fused_computation.7.clone.1 | convolution fusion | flops 66066248 | bytes 534336 | tf_op jit(solution)/shard_map/while/body/eval_jaxpr/bhqk,bkhe->bqhe/dot_general | solution.py:49
  68.7 2.7 %fusion.177 = bf16[6,1,250,8,32]{2,4,3,1,0:T(8,128)(2,1)} fusion(bf16[6,1,250,8,32]{2,4,3,1,0:T(8,128)(2,1)} %get-tuple-element.220, s32[]{:T(128)} %get-tuple-element.219, f32[8,250]{1,0:T(8,128)S(1)} %fusion.176, bf16[6,1,250,8,32]{2,4,3,1,0:T(8,128)(2,1)} %get-tuple-element.227, bf16[6,1,250,8,32]{2,4,3,1,0:T(8,128)(2,1)} %get-tuple-element.229, ...), kind=kOutput, calls=%fused_computation.7.clone.1 | convolution fusion | flops 66066248 | bytes 534336 | tf_op jit(solution)/shard_map/while/body/eval_jaxpr/bhqk,bkhe->bqhe/dot_general | solution.py:49
  71.4 1.8 fusion.176
  73.2 2.7 %fusion.177 = bf16[6,1,250,8,32]{2,4,3,1,0:T(8,128)(2,1)} fusion(bf16[6,1,250,8,32]{2,4,3,1,0:T(8,128)(2,1)} %get-tuple-element.220, s32[]{:T(128)} %get-tuple-element.219, f32[8,250]{1,0:T(8,128)S(1)} %fusion.176, bf16[6,1,250,8,32]{2,4,3,1,0:T(8,128)(2,1)} %get-tuple-element.227, bf16[6,1,250,8,32]{2,4,3,1,0:T(8,128)(2,1)} %get-tuple-element.229, ...), kind=kOutput, calls=%fused_computation.7.clone.1 | convolution fusion | flops 66066248 | bytes 534336 | tf_op jit(solution)/shard_map/while/body/eval_jaxpr/bhqk,bkhe->bqhe/dot_general | solution.py:49
  78.2 2.8 %fusion.105 = bf16[6,250,256]{2,1,0:T(8,128)(2,1)} fusion(bf16[6,250,256]{2,1,0:T(8,128)(2,1)S(1)} %get-tuple-element.144, bf16[1024,256,1]{1,0,2:T(8,128)(2,1)S(1)} %copy-done.10, bf16[256,1024,1]{0,1,2:T(8,128)(2,1)S(1)} %bitcast.240, f32[6,250]{1,0:T(8,128)S(1)} %add_rsqrt_fusion.1, f32[6,250]{1,0:T(8,128)S(1)} %broadcast_multiply_fusion.1), kind=kOutput, calls=%fused_computation.87 | convolution fusion | flops 1578624000 | bytes 2596576 | tf_op jit(solution)/shard_map/pcf,fd->pcd/dot_general | solution.py:84
  81.1 3.1 %reshape.243 = bf16[4,196608]{1,0:T(4,128)(2,1)} reshape(bf16[786432]{0:T(1024)(128)(2,1)} %all-gather.12.cloned.1.call-done) | data formatting | bytes 3145728 | tf_op jit(solution)/shard_map/all_gather | solution.py:19
  84.3 28.9 %all-gather.8.cloned.1.call-done = bf16[24,250,256]{2,1,0:T(8,128)(2,1)} async-done(((bf16[6,250,256]{2,1,0:T(8,128)(2,1)}), bf16[24,250,256]{2,1,0:T(8,128)(2,1)}) %all-gather.8.cloned.1.call-update) | async-done | bytes 3072016 | tf_op jit(solution)/shard_map/all_gather | solution.py:97
  113.2 2.1 pad.4
  115.3 3.2 %reshape.225 = bf16[32,4,2,24,256]{4,2,1,0,3:T(2,128)(2,1)} reshape(bf16[256,24,256]{2,0,1:T(8,128)(2,1)S(1)} %pad.4) | data formatting | bytes 6291456 | tf_op jit(solution)/shard_map/reshape | solution.py:103
  121.9 7.5 %all-to-all-start = ((bf16[64,24,256]{2,1,0:T(8,128)(2,1)}), bf16[64,24,256]{2,1,0:T(8,128)(2,1)S(1)}, u32[]{:S(2)}, u32[]{:S(2)}) async-start(bf16[64,24,256]{2,1,0:T(8,128)(2,1)} %bitcast.31), calls=%async_computation | async-start | bytes 1572864 | tf_op jit(solution)/shard_map/all_to_all | solution.py:108
  134.8 7.5 %all-to-all-done = bf16[64,24,256]{2,1,0:T(8,128)(2,1)S(1)} async-done(((bf16[64,24,256]{2,1,0:T(8,128)(2,1)}), bf16[64,24,256]{2,1,0:T(8,128)(2,1)S(1)}, u32[]{:S(2)}, u32[]{:S(2)}) %all-to-all-start) | async-done | bytes 786464 | tf_op jit(solution)/shard_map/all_to_all | solution.py:108
  144.8 36.6 %while.21 = (s32[]{:T(128)}, bf16[2,1,768,8,32]{2,4,3,1,0:T(8,128)(2,1)}, bf16[2,1,768,8,32]{2,4,3,1,0:T(8,128)(2,1)S(1)}, bf16[2,1,768,8,32]{2,4,3,1,0:T(8,128)...) while((s32[]{:T(128)}, bf16[2,1,768,8,32]{2,4,3,1,0:T(8,128)(2,1)}, ...), condition=%wide.region_13.14_spmd, body=%wide.region_10.13_spmd.sunk | while | flops 627770112 | bytes 39372868 | solution.py:62
  144.8 9.4 %fusion.181 = (f32[8,768]{1,0:T(8,128)S(1)}, f32[8,768,768]{1,2,0:T(8,128)}) fusion(bf16[2,1,768,8,32]{2,4,3,1,0:T(8,128)(2,1)S(1)} %get-tuple-element.247, s32[]{:T(128)} %get-tuple-element.237, bf16[2,1,768,8,32]{2,4,3,1,0:T(8,128)(2,1)S(1)} %get-tuple-element.246), kind=kOutput, calls=%fused_computation.123.clone.1 | convolution fusion | flops 316146432 | bytes 19686400 | tf_op jit(solution)/shard_map/while/body/eval_jaxpr/sub | solution.py:46
  154.2 8.8 %fusion.182 = bf16[2,1,768,8,32]{2,4,3,1,0:T(8,128)(2,1)} fusion(bf16[2,1,768,8,32]{2,4,3,1,0:T(8,128)(2,1)} %get-tuple-element.238, s32[]{:T(128)} %get-tuple-element.237, f32[8,768,768]{1,2,0:T(8,128)} %get-tuple-element.211, f32[8,768]{1,0:T(8,128)S(1)} %get-tuple-element.212, bf16[2,1,768,8,32]{2,4,3,1,0:T(8,128)(2,1)S(1)} %get-tuple-element.245), kind=kOutput, calls=%fused_computation.37.clone.1 | convolution fusion | flops 311623680 | bytes 19686400 | tf_op jit(solution)/shard_map/while/body/eval_jaxpr/bhqk,bkhe->bqhe/dot_general | solution.py:49
  163.1 9.4 %fusion.181 = (f32[8,768]{1,0:T(8,128)S(1)}, f32[8,768,768]{1,2,0:T(8,128)}) fusion(bf16[2,1,768,8,32]{2,4,3,1,0:T(8,128)(2,1)S(1)} %get-tuple-element.247, s32[]{:T(128)} %get-tuple-element.237, bf16[2,1,768,8,32]{2,4,3,1,0:T(8,128)(2,1)S(1)} %get-tuple-element.246), kind=kOutput, calls=%fused_computation.123.clone.1 | convolution fusion | flops 316146432 | bytes 19686400 | tf_op jit(solution)/shard_map/while/body/eval_jaxpr/sub | solution.py:46
  172.5 8.9 %fusion.182 = bf16[2,1,768,8,32]{2,4,3,1,0:T(8,128)(2,1)} fusion(bf16[2,1,768,8,32]{2,4,3,1,0:T(8,128)(2,1)} %get-tuple-element.238, s32[]{:T(128)} %get-tuple-element.237, f32[8,768,768]{1,2,0:T(8,128)} %get-tuple-element.211, f32[8,768]{1,0:T(8,128)S(1)} %get-tuple-element.212, bf16[2,1,768,8,32]{2,4,3,1,0:T(8,128)(2,1)S(1)} %get-tuple-element.245), kind=kOutput, calls=%fused_computation.37.clone.1 | convolution fusion | flops 311623680 | bytes 19686400 | tf_op jit(solution)/shard_map/while/body/eval_jaxpr/bhqk,bkhe->bqhe/dot_general | solution.py:49
  184.1 1.9 fusion.106
  186.6 17.8 %all_to_all.24 = bf16[2,768,256]{2,0,1:T(2,128)(2,1)S(1)} all-to-all(bf16[2,768,256]{2,0,1:T(2,128)(2,1)S(1)} %copy.119), channel_id=1, replica_groups=mesh['seq'=32,'mp'=4] {'seq'}, dimensions={1} | all-to-all | bytes 1572864 | tf_op jit(solution)/shard_map/all_to_all | solution.py:112
  205.4 31.4 %all-gather.14.cloned.1.call-done = bf16[32,8,24,256]{3,2,0,1:T(8,128)(2,1)} async-done(((bf16[32,2,24,256]{3,2,0,1:T(8,128)(2,1)}), bf16[32,8,24,256]{3,2,0,1:T(8,128)(2,1)}) %all-gather.14.cloned.1.call-update) | async-done | bytes 3145744 | tf_op jit(solution)/shard_map/all_gather | solution.py:114
  236.8 2.3 copy.121
  239.5 2.6 collective-permute-start
  242.1 6.5 %collective-permute-done = bf16[125,256]{1,0:T(8,128)(2,1)S(1)} collective-permute-done((bf16[125,256]{1,0:T(8,128)(2,1)S(1)}, bf16[125,256]{1,0:T(8,128)(2,1)S(1)}, u32[]{:S(2)}, u32[]{:S(2)}) %collective-permute-start) | collective-permute-done | bytes 64032 | tf_op jit(solution)/shard_map/ppermute | solution.py:30
  251.3 2.7 %reshape.238 = bf16[3000,256]{1,0:T(8,128)(2,1)} reshape(bf16[24,125,256]{2,1,0:T(8,128)(2,1)} %copy.123) | data formatting | bytes 3072000 | tf_op jit(solution)/shard_map/reshape | solution.py:122
  (107 shorter events, 43.9 us)
Async XLA Ops:
  6.5 9.1 %copy-start = (bf16[24,250,256]{2,0,1:T(8,128)(2,1)S(1)}, bf16[24,250,256]{2,0,1:T(8,128)(2,1)}, u32[]{:S(2)}) copy-start(bf16[24,250,256]{2,0,1:T(8,128)(2,1)} %param.13) | copy-start | bytes 9216004
  6.5 5.1 %copy-start.11 = (bf16[256,3,64]{0,2,1:T(8,128)(2,1)S(1)}, bf16[256,3,64]{0,2,1:T(8,128)(2,1)}, u32[]{:S(2)}) copy-start(bf16[256,3,64]{0,2,1:T(8,128)(2,1)} %param.18) | copy-start | bytes 294916
  6.5 31.3 %all-gather.10.cloned.1.call-start = ((), (), s32[]{:S(2)}) async-start(), calls=%async_computation.3 | async-start | bytes 1966080 | tf_op jit(solution)/shard_map/all_gather | solution.py:19
  11.5 69.6 %all-gather.12.cloned.1.call-start = ((), (), s32[]{:S(2)}) async-start(), calls=%async_computation.4 | async-start | bytes 1966080 | tf_op jit(solution)/shard_map/all_gather | solution.py:19
  15.6 97.6 %all-gather.8.cloned.1.call-start = ((), (), s32[]{:S(2)}) async-start(), calls=%async_computation.2 | async-start | bytes 3932160 | tf_op jit(solution)/shard_map/all_gather | solution.py:97
  15.9 1.0 copy-start.2
  39.8 1.4 copy-start.5
  41.2 3.2 %copy-start.3 = (bf16[6,250,256]{2,0,1:T(8,128)(2,1)S(1)}, bf16[6,250,256]{2,0,1:T(8,128)(2,1)}, u32[]{:S(2)}) copy-start(bf16[6,250,256]{2,0,1:T(8,128)(2,1)} %copy-done.2) | copy-start | bytes 2304004
  45.4 1.5 slice-start.2
  45.4 1.6 copy-start.6
  76.0 2.3 copy-start.10
  120.3 9.3 %copy-start.4 = (bf16[4,196608]{1,0:T(4,128)(2,1)S(1)}, bf16[4,196608]{1,0:T(4,128)(2,1)}, u32[]{:S(2)}) copy-start(bf16[4,196608]{1,0:T(4,128)(2,1)} %reshape.243) | copy-start | bytes 4718596
  121.9 20.4 %all-to-all-start = ((bf16[64,24,256]{2,1,0:T(8,128)(2,1)}), bf16[64,24,256]{2,1,0:T(8,128)(2,1)S(1)}, u32[]{:S(2)}, u32[]{:S(2)}) async-start(bf16[64,24,256]{2,1,0:T(8,128)(2,1)} %bitcast.31), calls=%async_computation | async-start | bytes 1572864 | tf_op jit(solution)/shard_map/all_to_all | solution.py:108
  129.4 1.4 slice-start
  129.4 107.4 %all-gather.14.cloned.1.call-start = ((), (), s32[]{:S(2)}) async-start(), calls=%async_computation.5 | async-start | bytes 3932160 | tf_op jit(solution)/shard_map/all_gather | solution.py:114
  130.8 1.3 slice-start.1
  131.5 1.1 copy-start.7
  182.2 1.9 copy-start.8
  182.2 1.9 copy-start.9
  239.5 9.2 %collective-permute-start = (bf16[125,256]{1,0:T(8,128)(2,1)S(1)}, bf16[125,256]{1,0:T(8,128)(2,1)S(1)}, u32[]{:S(2)}, u32[]{:S(2)}) collective-permute-start(bf16[125,256]{1,0:T(8,128)(2,1)S(1)} %bitcast.251), channel_id=1, source_target_pairs={{0,4},{4,8},{8,12},{12,16},{16,20},{20,24},{24,28},{28,32},{32,36}... | collective-permute-start | bytes 192008 | tf_op jit(solution)/shard_map/ppermute | solution.py:30
  249.8 4.2 %copy-start.1 = (bf16[24,250,256]{2,0,1:T(8,128)(2,1)S(1)}, bf16[24,250,256]{2,0,1:T(8,128)(2,1)}, u32[]{:S(2)}) copy-start(bf16[24,250,256]{2,0,1:T(8,128)(2,1)} %param.13) | copy-start | bytes 9216004
Sparse Core Ops, SparseCore 0:
  11.7 26.1 all-gather.9
  39.5 23.1 all-gather.11
  81.2 31.9 all-gather.7
  205.6 31.2 all-gather.13
where the time goes:
time: 262 us; the launch traced here: 261 us
  waiting for transfers between devices  94.7 us (36%)
  matrix products  73.9 us (28%)
  local copies, waits for them, and re-layouts  44.2 us (17%)
  blocking collectives  17.8 us (7%)
  between operations  13.7 us (5%)
  starting transfers between devices  10.4 us (4%)
  other arithmetic  5.78 us (2%)
    dot_general x8, matrix products, attend(): jnp.einsum('bhqk,bkhe->bqhe', weights, value_rows, preferred_element_type...  34.2 us
    all_gather x1, waiting for transfers between devices, on_device(): collected = lax.all_gather(returned, 'mp', axis=1, tiled=True)  31.4 us
    sub x8, matrix products, attend(): scores = scores - jnp.max(scores, axis=-1, keepdims=True)  29.9 us
    all_gather x1, waiting for transfers between devices, on_device(): stream = lax.all_gather(finished, 'mp', axis=0, tiled=True)  28.9 us
    all_gather x2, waiting for transfers between devices, gather_together(): lines, at, done = (lax.all_gather(vector, axis), 0, [])  20.4 us
    all_to_all x1, blocking collectives, on_device(): lax.all_to_all(spread_rows, 'seq', split_axis=1, concat_axis=0, tiled=True)  17.8 us
    unnamed x36, local copies, waits for them, and re-layouts  9.77 us
    all_to_all x1, starting transfers between devices, on_device(): lax.all_to_all(mine, 'seq', split_axis=0, concat_axis=1, tiled=True)  7.49 us
  transfers between devices with their start and end apart: 6, of which 5 were waited for; matrix products, arithmetic and copies ran while one was open for 22% of the time, Pallas kernels for 0%

commit v1 on v0

--- a/solution.py
+++ b/solution.py
@@ -2,6 +2,7 @@
 import jax.numpy as jnp
 from jax import lax
 from jax.sharding import PartitionSpec as P
+from jax.lax import all_to_all, axis_size
 
 HEADS = 8
 HD = 32
@@ -111,7 +112,15 @@
     )
     returned = lax.all_to_all(spread_rows, "seq", split_axis=1, concat_axis=0, tiled=True)
     returned = returned.reshape(seq_count, 1, per_device, stream.shape[0], stream.shape[2])
-    collected = lax.all_gather(returned, "mp", axis=1, tiled=True)
+    collected = jnp.concatenate(
+        all_to_all(
+            jnp.stack(axis_size("mp") * [returned], axis=0),
+            axis_name="mp",
+            split_axis=0,
+            concat_axis=0,
+        ),
+        axis=1,
+    )
     collected = collected.reshape(padded_len, stream.shape[0], stream.shape[2])
     stream = jnp.transpose(collected[:K], (1, 0, 2))
     hop_len = K // 2

time: 262 us -> 276 us (1.053)
  blocking collectives: 17.8 us -> 59.2 us
  waiting for transfers between devices: 94.7 us -> 63.3 us
  local copies, waits for them, and re-layouts: 44.2 us -> 48.4 us
    all_to_all x0 -> x1, blocking collectives: none -> 41.4 us  [on_device(): all_to_all(jnp.stack(axis_size('mp') * [returned], axis=0), axis_name='mp...]
    all_gather x1 -> x0, waiting for transfers between devices: 31.4 us -> none  [on_device(): collected = lax.all_gather(returned, 'mp', axis=1, tiled=True)]
    all_to_all x0 -> x1, local copies, waits for them, and re-layouts: none -> 3.39 us  [on_device(): all_to_all(jnp.stack(axis_size('mp') * [returned], axis=0), axis_name='mp...]
    another operation x0 -> x1, local copies, waits for them, and re-layouts: none -> 3.1 us  [on_device(): jnp.stack(axis_size('mp') * [returned], axis=0)]
  transfers between devices with their start and end apart: 6 -> 5, of which waited for: 5 -> 4; matrix products, arithmetic and copies ran while one was open for 22% -> 20% of each run, Pallas kernels for 0% -> 0%
where the time goes in v1:
time: 276 us; the launch traced here: 275 us
  matrix products  74 us (27%)
  waiting for transfers between devices  63.3 us (23%)
  blocking collectives  59.2 us (21%)
  local copies, waits for them, and re-layouts  48.4 us (18%)
  between operations  13.7 us (5%)
  starting transfers between devices  10.4 us (4%)
  other arithmetic  5.78 us (2%)
    all_to_all x1, blocking collectives, on_device(): all_to_all(jnp.stack(axis_size('mp') * [returned], axis=0), axis_name='mp...  41.4 us
    dot_general x8, matrix products, attend(): jnp.einsum('bhqk,bkhe->bqhe', weights, value_rows, preferred_element_type...  34.2 us
    sub x8, matrix products, attend(): scores = scores - jnp.max(scores, axis=-1, keepdims=True)  29.9 us
    all_gather x1, waiting for transfers between devices, on_device(): stream = lax.all_gather(finished, 'mp', axis=0, tiled=True)  28.9 us
    all_gather x2, waiting for transfers between devices, gather_together(): lines, at, done = (lax.all_gather(vector, axis), 0, [])  20.4 us
    all_to_all x1, blocking collectives, on_device(): lax.all_to_all(spread_rows, 'seq', split_axis=1, concat_axis=0, tiled=True)  17.8 us
    unnamed x36, local copies, waits for them, and re-layouts  9.76 us
    all_to_all x1, waiting for transfers between devices, on_device(): lax.all_to_all(mine, 'seq', split_axis=0, concat_axis=1, tiled=True)  7.66 us
  transfers between devices with their start and end apart: 5, of which 4 were waited for; matrix products, arithmetic and copies ran while one was open for 20% of the time, Pallas kernels for 0%

profile of v1, /device:TPU:8, one launch (start us, length us, event | category | flops | bytes accessed | tf_op | source)
XLA Modules:
  0.0 274.8 jit_solution(2454683857177244326)
XLA Ops:
  17.4 20.4 %all-gather.8.cloned.1.call-done = bf16[786432]{0:T(1024)(128)(2,1)} async-done(((bf16[196608]{0:T(1024)(128)(2,1)}), bf16[786432]{0:T(1024)(128)(2,1)}) %all-gather.8.cloned.1.call-update) | async-done | bytes 1572880 | tf_op jit(solution)/shard_map/all_gather | solution.py:20
  37.8 2.0 reshape.240
  48.4 27.6 %while.20 = (s32[]{:T(128)}, bf16[6,1,250,8,32]{2,4,3,1,0:T(8,128)(2,1)}, bf16[6,1,250,8,32]{2,4,3,1,0:T(8,128)(2,1)}, bf16[6,1,250,8,32]{2,4,3,1,0:T(8,128)(2,1...) while((s32[]{:T(128)}, bf16[6,1,250,8,32]{2,4,3,1,0:T(8,128)(2,1)}, bf16[6,1,250,8,32]{2,4,3,1,0:T(8,128)(2,1)}, ...), condition=%wide.region_5.6_spmd, body=%wide.region_2.5_spmd.sunk | while | flops 99566496 | bytes 805573 | solution.py:63
  48.4 1.8 fusion.176
  50.3 2.8 %fusion.177 = bf16[6,1,250,8,32]{2,4,3,1,0:T(8,128)(2,1)} fusion(bf16[6,1,250,8,32]{2,4,3,1,0:T(8,128)(2,1)} %get-tuple-element.240, s32[]{:T(128)} %get-tuple-element.239, f32[8,250]{1,0:T(8,128)S(1)} %fusion.176, bf16[6,1,250,8,32]{2,4,3,1,0:T(8,128)(2,1)} %get-tuple-element.247, bf16[6,1,250,8,32]{2,4,3,1,0:T(8,128)(2,1)} %get-tuple-element.249, ...), kind=kOutput, calls=%fused_computation.7.clone.1 | convolution fusion | flops 66066248 | bytes 534336 | tf_op jit(solution)/shard_map/while/body/eval_jaxpr/bhqk,bkhe->bqhe/dot_general | solution.py:50
  53.1 1.8 fusion.176
  54.9 2.8 %fusion.177 = bf16[6,1,250,8,32]{2,4,3,1,0:T(8,128)(2,1)} fusion(bf16[6,1,250,8,32]{2,4,3,1,0:T(8,128)(2,1)} %get-tuple-element.240, s32[]{:T(128)} %get-tuple-element.239, f32[8,250]{1,0:T(8,128)S(1)} %fusion.176, bf16[6,1,250,8,32]{2,4,3,1,0:T(8,128)(2,1)} %get-tuple-element.247, bf16[6,1,250,8,32]{2,4,3,1,0:T(8,128)(2,1)} %get-tuple-element.249, ...), kind=kOutput, calls=%fused_computation.7.clone.1 | convolution fusion | flops 66066248 | bytes 534336 | tf_op jit(solution)/shard_map/while/body/eval_jaxpr/bhqk,bkhe->bqhe/dot_general | solution.py:50
  57.7 1.8 fusion.176
  59.5 2.8 %fusion.177 = bf16[6,1,250,8,32]{2,4,3,1,0:T(8,128)(2,1)} fusion(bf16[6,1,250,8,32]{2,4,3,1,0:T(8,128)(2,1)} %get-tuple-element.240, s32[]{:T(128)} %get-tuple-element.239, f32[8,250]{1,0:T(8,128)S(1)} %fusion.176, bf16[6,1,250,8,32]{2,4,3,1,0:T(8,128)(2,1)} %get-tuple-element.247, bf16[6,1,250,8,32]{2,4,3,1,0:T(8,128)(2,1)} %get-tuple-element.249, ...), kind=kOutput, calls=%fused_computation.7.clone.1 | convolution fusion | flops 66066248 | bytes 534336 | tf_op jit(solution)/shard_map/while/body/eval_jaxpr/bhqk,bkhe->bqhe/dot_general | solution.py:50
  64.1 2.8 %fusion.177 = bf16[6,1,250,8,32]{2,4,3,1,0:T(8,128)(2,1)} fusion(bf16[6,1,250,8,32]{2,4,3,1,0:T(8,128)(2,1)} %get-tuple-element.240, s32[]{:T(128)} %get-tuple-element.239, f32[8,250]{1,0:T(8,128)S(1)} %fusion.176, bf16[6,1,250,8,32]{2,4,3,1,0:T(8,128)(2,1)} %get-tuple-element.247, bf16[6,1,250,8,32]{2,4,3,1,0:T(8,128)(2,1)} %get-tuple-element.249, ...), kind=kOutput, calls=%fused_computation.7.clone.1 | convolution fusion | flops 66066248 | bytes 534336 | tf_op jit(solution)/shard_map/while/body/eval_jaxpr/bhqk,bkhe->bqhe/dot_general | solution.py:50
  68.7 2.7 fusion.177
  73.3 2.8 %fusion.177 = bf16[6,1,250,8,32]{2,4,3,1,0:T(8,128)(2,1)} fusion(bf16[6,1,250,8,32]{2,4,3,1,0:T(8,128)(2,1)} %get-tuple-element.240, s32[]{:T(128)} %get-tuple-element.239, f32[8,250]{1,0:T(8,128)S(1)} %fusion.176, bf16[6,1,250,8,32]{2,4,3,1,0:T(8,128)(2,1)} %get-tuple-element.247, bf16[6,1,250,8,32]{2,4,3,1,0:T(8,128)(2,1)} %get-tuple-element.249, ...), kind=kOutput, calls=%fused_computation.7.clone.1 | convolution fusion | flops 66066248 | bytes 534336 | tf_op jit(solution)/shard_map/while/body/eval_jaxpr/bhqk,bkhe->bqhe/dot_general | solution.py:50
  78.3 2.8 %fusion.105 = bf16[6,250,256]{2,1,0:T(8,128)(2,1)} fusion(bf16[6,250,256]{2,1,0:T(8,128)(2,1)S(1)} %get-tuple-element.164, bf16[1024,256,1]{1,0,2:T(8,128)(2,1)S(1)} %copy-done.10, bf16[256,1024,1]{0,1,2:T(8,128)(2,1)S(1)} %bitcast.242, f32[6,250]{1,0:T(8,128)S(1)} %add_rsqrt_fusion.1, f32[6,250]{1,0:T(8,128)S(1)} %broadcast_multiply_fusion.1), kind=kOutput, calls=%fused_computation.87 | convolution fusion | flops 1578624000 | bytes 2596576 | tf_op jit(solution)/shard_map/pcf,fd->pcd/dot_general | solution.py:85
  81.2 3.2 %reshape.241 = bf16[4,196608]{1,0:T(4,128)(2,1)} reshape(bf16[786432]{0:T(1024)(128)(2,1)} %all-gather.10.cloned.1.call-done) | data formatting | bytes 3145728 | tf_op jit(solution)/shard_map/all_gather | solution.py:20
  84.4 28.9 %all-gather.6.cloned.1.call-done = bf16[24,250,256]{2,1,0:T(8,128)(2,1)} async-done(((bf16[6,250,256]{2,1,0:T(8,128)(2,1)}), bf16[24,250,256]{2,1,0:T(8,128)(2,1)}) %all-gather.6.cloned.1.call-update) | async-done | bytes 3072016 | tf_op jit(solution)/shard_map/all_gather | solution.py:98
  113.3 2.1 pad.4
  115.4 3.2 %reshape.224 = bf16[32,4,2,24,256]{4,2,1,0,3:T(2,128)(2,1)} reshape(bf16[256,24,256]{2,0,1:T(8,128)(2,1)S(1)} %pad.4) | data formatting | bytes 6291456 | tf_op jit(solution)/shard_map/reshape | solution.py:104
  121.9 7.5 %all-to-all-start = ((bf16[64,24,256]{2,1,0:T(8,128)(2,1)}), bf16[64,24,256]{2,1,0:T(8,128)(2,1)S(1)}, u32[]{:S(2)}, u32[]{:S(2)}) async-start(bf16[64,24,256]{2,1,0:T(8,128)(2,1)} %bitcast.31), calls=%async_computation | async-start | bytes 1572864 | tf_op jit(solution)/shard_map/all_to_all | solution.py:109
  134.7 7.7 %all-to-all-done = bf16[64,24,256]{2,1,0:T(8,128)(2,1)S(1)} async-done(((bf16[64,24,256]{2,1,0:T(8,128)(2,1)}), bf16[64,24,256]{2,1,0:T(8,128)(2,1)S(1)}, u32[]{:S(2)}, u32[]{:S(2)}) %all-to-all-start) | async-done | bytes 786464 | tf_op jit(solution)/shard_map/all_to_all | solution.py:109
  144.8 36.6 %while.21 = (s32[]{:T(128)}, bf16[2,1,768,8,32]{2,4,3,1,0:T(8,128)(2,1)}, bf16[2,1,768,8,32]{2,4,3,1,0:T(8,128)(2,1)S(1)}, bf16[2,1,768,8,32]{2,4,3,1,0:T(8,128)...) while((s32[]{:T(128)}, bf16[2,1,768,8,32]{2,4,3,1,0:T(8,128)(2,1)}, ...), condition=%wide.region_13.14_spmd, body=%wide.region_10.13_spmd.sunk | while | flops 627770112 | bytes 39372868 | solution.py:63
  144.9 9.5 %fusion.181 = (f32[8,768]{1,0:T(8,128)S(1)}, f32[8,768,768]{1,2,0:T(8,128)}) fusion(bf16[2,1,768,8,32]{2,4,3,1,0:T(8,128)(2,1)S(1)} %get-tuple-element.267, s32[]{:T(128)} %get-tuple-element.257, bf16[2,1,768,8,32]{2,4,3,1,0:T(8,128)(2,1)S(1)} %get-tuple-element.266), kind=kOutput, calls=%fused_computation.123.clone.1 | convolution fusion | flops 316146432 | bytes 19686400 | tf_op jit(solution)/shard_map/while/body/eval_jaxpr/sub | solution.py:47
  154.3 8.9 %fusion.182 = bf16[2,1,768,8,32]{2,4,3,1,0:T(8,128)(2,1)} fusion(bf16[2,1,768,8,32]{2,4,3,1,0:T(8,128)(2,1)} %get-tuple-element.258, s32[]{:T(128)} %get-tuple-element.257, f32[8,768,768]{1,2,0:T(8,128)} %get-tuple-element.231, f32[8,768]{1,0:T(8,128)S(1)} %get-tuple-element.232, bf16[2,1,768,8,32]{2,4,3,1,0:T(8,128)(2,1)S(1)} %get-tuple-element.265), kind=kOutput, calls=%fused_computation.37.clone.1 | convolution fusion | flops 311623680 | bytes 19686400 | tf_op jit(solution)/shard_map/while/body/eval_jaxpr/bhqk,bkhe->bqhe/dot_general | solution.py:50
  163.2 9.4 %fusion.181 = (f32[8,768]{1,0:T(8,128)S(1)}, f32[8,768,768]{1,2,0:T(8,128)}) fusion(bf16[2,1,768,8,32]{2,4,3,1,0:T(8,128)(2,1)S(1)} %get-tuple-element.267, s32[]{:T(128)} %get-tuple-element.257, bf16[2,1,768,8,32]{2,4,3,1,0:T(8,128)(2,1)S(1)} %get-tuple-element.266), kind=kOutput, calls=%fused_computation.123.clone.1 | convolution fusion | flops 316146432 | bytes 19686400 | tf_op jit(solution)/shard_map/while/body/eval_jaxpr/sub | solution.py:47
  172.6 8.9 %fusion.182 = bf16[2,1,768,8,32]{2,4,3,1,0:T(8,128)(2,1)} fusion(bf16[2,1,768,8,32]{2,4,3,1,0:T(8,128)(2,1)} %get-tuple-element.258, s32[]{:T(128)} %get-tuple-element.257, f32[8,768,768]{1,2,0:T(8,128)} %get-tuple-element.231, f32[8,768]{1,0:T(8,128)S(1)} %get-tuple-element.232, bf16[2,1,768,8,32]{2,4,3,1,0:T(8,128)(2,1)S(1)} %get-tuple-element.265), kind=kOutput, calls=%fused_computation.37.clone.1 | convolution fusion | flops 311623680 | bytes 19686400 | tf_op jit(solution)/shard_map/while/body/eval_jaxpr/bhqk,bkhe->bqhe/dot_general | solution.py:50
  184.2 1.9 fusion.106
  186.8 17.8 %all_to_all.29 = bf16[2,768,256]{2,0,1:T(2,128)(2,1)S(1)} all-to-all(bf16[2,768,256]{2,0,1:T(2,128)(2,1)S(1)} %copy.173), channel_id=1, replica_groups=mesh['seq'=32,'mp'=4] {'seq'}, dimensions={1} | all-to-all | bytes 1572864 | tf_op jit(solution)/shard_map/all_to_all | solution.py:113
  205.5 3.1 %stack.3 = bf16[4,32,1,2,24,256]{5,3,1,4,2,0:T(2,128)(2,1)S(1)} broadcast(bf16[32,2,24,256]{3,1,0,2:T(2,128)(2,1)S(1)} %copy.175), dimensions={1,3,4,5} | broadcast | bytes 3932160 | tf_op jit(solution)/shard_map/stack | solution.py:117
  208.6 41.4 %all_to_all.30 = bf16[4,32,1,2,24,256]{5,3,1,4,2,0:T(2,128)(2,1)S(1)} all-to-all(bf16[4,32,1,2,24,256]{5,3,1,4,2,0:T(2,128)(2,1)S(1)} %stack.3), channel_id=1, replica_groups=mesh['seq'=32,'mp'=4] {'mp'}, dimensions={0} | all-to-all | bytes 6291456 | tf_op jit(solution)/shard_map/all_to_all | solution.py:116
  250.0 3.4 %copy.176 = bf16[4,32,1,2,24,256]{5,4,3,0,1,2:T(8,128)(2,1)S(1)} copy(bf16[4,32,1,2,24,256]{5,3,1,4,2,0:T(2,128)(2,1)S(1)} %all_to_all.30) | data formatting | bytes 6291456 | tf_op jit(solution)/shard_map/all_to_all | solution.py:116
  253.8 2.8 %collective-permute-start = (bf16[125,256]{1,0:T(8,128)(2,1)S(1)}, bf16[125,256]{1,0:T(8,128)(2,1)S(1)}, u32[]{:S(2)}, u32[]{:S(2)}) collective-permute-start(bf16[125,256]{1,0:T(8,128)(2,1)S(1)} %bitcast.253), channel_id=1, source_target_pairs={{0,4},{4,8},{8,12},{12,16},{16,20},{20,24},{24,28},{28,32},{32,36}... | collective-permute-start | bytes 192008 | tf_op jit(solution)/shard_map/ppermute | solution.py:31
  256.7 6.2 %collective-permute-done = bf16[125,256]{1,0:T(8,128)(2,1)S(1)} collective-permute-done((bf16[125,256]{1,0:T(8,128)(2,1)S(1)}, bf16[125,256]{1,0:T(8,128)(2,1)S(1)}, u32[]{:S(2)}, u32[]{:S(2)}) %collective-permute-start) | collective-permute-done | bytes 64032 | tf_op jit(solution)/shard_map/ppermute | solution.py:31
  265.6 2.7 reshape.236
  (107 shorter events, 45.4 us)
Async XLA Ops:
  6.5 9.1 %copy-start = (bf16[24,250,256]{2,0,1:T(8,128)(2,1)S(1)}, bf16[24,250,256]{2,0,1:T(8,128)(2,1)}, u32[]{:S(2)}) copy-start(bf16[24,250,256]{2,0,1:T(8,128)(2,1)} %param.13) | copy-start | bytes 9216004
  6.5 5.1 %copy-start.11 = (bf16[256,3,64]{0,2,1:T(8,128)(2,1)S(1)}, bf16[256,3,64]{0,2,1:T(8,128)(2,1)}, u32[]{:S(2)}) copy-start(bf16[256,3,64]{0,2,1:T(8,128)(2,1)} %param.18) | copy-start | bytes 294916
  6.5 31.3 %all-gather.8.cloned.1.call-start = ((), (), s32[]{:S(2)}) async-start(), calls=%async_computation.4 | async-start | bytes 1966080 | tf_op jit(solution)/shard_map/all_gather | solution.py:20
  11.5 69.7 %all-gather.10.cloned.1.call-start = ((), (), s32[]{:S(2)}) async-start(), calls=%async_computation.5 | async-start | bytes 1966080 | tf_op jit(solution)/shard_map/all_gather | solution.py:20
  15.6 97.7 %all-gather.6.cloned.1.call-start = ((), (), s32[]{:S(2)}) async-start(), calls=%async_computation.3 | async-start | bytes 3932160 | tf_op jit(solution)/shard_map/all_gather | solution.py:98
  15.9 1.0 copy-start.2
  39.8 1.4 copy-start.5
  41.2 3.2 %copy-start.3 = (bf16[6,250,256]{2,0,1:T(8,128)(2,1)S(1)}, bf16[6,250,256]{2,0,1:T(8,128)(2,1)}, u32[]{:S(2)}) copy-start(bf16[6,250,256]{2,0,1:T(8,128)(2,1)} %copy-done.2) | copy-start | bytes 2304004
  45.4 1.5 slice-start.2
  45.4 1.6 copy-start.6
  76.0 2.3 copy-start.10
  120.4 9.1 %copy-start.4 = (bf16[4,196608]{1,0:T(4,128)(2,1)S(1)}, bf16[4,196608]{1,0:T(4,128)(2,1)}, u32[]{:S(2)}) copy-start(bf16[4,196608]{1,0:T(4,128)(2,1)} %reshape.241) | copy-start | bytes 4718596
  121.9 20.4 %all-to-all-start = ((bf16[64,24,256]{2,1,0:T(8,128)(2,1)}), bf16[64,24,256]{2,1,0:T(8,128)(2,1)S(1)}, u32[]{:S(2)}, u32[]{:S(2)}) async-start(bf16[64,24,256]{2,1,0:T(8,128)(2,1)} %bitcast.31), calls=%async_computation | async-start | bytes 1572864 | tf_op jit(solution)/shard_map/all_to_all | solution.py:109
  129.5 1.2 slice-start
  130.6 1.3 slice-start.1
  131.4 1.1 copy-start.7
  182.3 1.9 copy-start.8
  182.3 1.9 copy-start.9
  253.8 9.2 %collective-permute-start = (bf16[125,256]{1,0:T(8,128)(2,1)S(1)}, bf16[125,256]{1,0:T(8,128)(2,1)S(1)}, u32[]{:S(2)}, u32[]{:S(2)}) collective-permute-start(bf16[125,256]{1,0:T(8,128)(2,1)S(1)} %bitcast.253), channel_id=1, source_target_pairs={{0,4},{4,8},{8,12},{12,16},{16,20},{20,24},{24,28},{28,32},{32,36}... | collective-permute-start | bytes 192008 | tf_op jit(solution)/shard_map/ppermute | solution.py:31
  264.1 4.2 %copy-start.1 = (bf16[24,250,256]{2,0,1:T(8,128)(2,1)S(1)}, bf16[24,250,256]{2,0,1:T(8,128)(2,1)}, u32[]{:S(2)}) copy-start(bf16[24,250,256]{2,0,1:T(8,128)(2,1)} %param.13) | copy-start | bytes 9216004
Sparse Core Ops, SparseCore 0:
  11.7 26.1 all-gather.7
  39.5 23.0 all-gather.9
  81.3 31.9 all-gather.5
